TPU v7x, 256 devices: a whole 4x4x8 slice. The times are simulated.
256 devices in a mesh: expert: 32 (over z, y), etp: 8 (over x, core).
Axes of the slice: x: 4, y: 4, z: 8, core: 2. Of those that a mesh axis runs over, the one named last changes fastest.
Arguments:
- tokens: bfloat16 [32768, 2560], P(('expert', 'etp')), may hold values from -6 to 6
- grad_out: bfloat16 [32768, 2560], P(('expert', 'etp')), may hold values from -6 to 6
- router_weight: bfloat16 [2560, 32], replicated, may hold values from -0.125 to 0.125
- expert_choice: int32 [32768, 1], P(('expert', 'etp')), may hold values from 0 to 31; in each aligned block of 128 rows (0 to 127, 128 to 255, ...) at most 6 rows name the same one
- gate_pre: bfloat16 [32, 1536, 4096], P('expert', None, 'etp'), may hold values from -6 to 6
- up_pre: bfloat16 [32, 1536, 4096], P('expert', None, 'etp'), may hold values from -6 to 6
- w_gate: bfloat16 [32, 2560, 4096], P('expert', None, 'etp'), may hold values from -0.125 to 0.125
- w_up: bfloat16 [32, 2560, 4096], P('expert', None, 'etp'), may hold values from -0.125 to 0.125
- w_down: bfloat16 [32, 4096, 2560], P('expert', 'etp'), may hold values from -0.09375 to 0.09375
Outputs:
- token_grad: bfloat16 [32768, 2560], P(('expert', 'etp'))
- router_grad: float32 [2560, 32], replicated
Inputs may be any that keep to these rules, and one draw needn't show every extreme that they name: `expert_choice`: within the 128 tokens of one device no expert is chosen more than 6 times, and in every draw some expert is chosen exactly 6 times by the tokens of some device.
All inputs are finite; a program needn't handle non-finite values.
Results may differ from a plain program's by a relative error of at most 0.015.
Values may be sent and summed in bfloat16 or wider, within the bound.
No kernel may reach another device: no remote copies, remote signals or barrier semaphores. Data moves between devices by JAX's collectives and lax.ppermute only.
A program may use at most 128 MiB of HBM per device.

v0:
```python
import jax
import jax.numpy as jnp
from jax import lax
from jax.sharding import PartitionSpec as P


def local(tokens, grad_out, router_weight, expert_choice, gate_pre, up_pre, w_gate, w_up, w_down):
    width = tokens.shape[1]
    experts = router_weight.shape[1]
    n_expert = lax.axis_size("expert")
    n_etp = lax.axis_size("etp")
    capacity = gate_pre.shape[1] // (n_expert * n_etp)
    hidden = w_down.shape[1]
    contract = (((1,), (1,)), ((), ()))
    chosen_ids = expert_choice[:, 0]
    picked = chosen_ids[:, None] == jnp.arange(experts, dtype=jnp.int32)[None, :]
    logits = jnp.dot(tokens, router_weight, preferred_element_type=jnp.float32)
    score = jax.nn.sigmoid(jnp.sum(jnp.where(picked, logits, 0.0), axis=1))
    counts = picked.astype(jnp.int32)
    earlier = jnp.cumsum(counts, axis=0) - counts
    position = jnp.sum(earlier * counts, axis=1)
    target = chosen_ids * capacity + position
    outgoing = jnp.zeros((experts * capacity, width), jnp.bfloat16).at[target].set(grad_out)
    gate_all = gate_pre[0]
    up_all = up_pre[0]
    gate_w = w_gate[0]
    up_w = w_up[0]
    down_w = w_down[0]
    pooled = lax.all_gather(outgoing, "etp", axis=0, tiled=True)
    pooled = pooled.reshape(n_etp, experts * capacity, width)
    arrived = lax.all_to_all(pooled, "expert", split_axis=1, concat_axis=1, tiled=True)
    d_hidden = lax.dot_general(
        arrived.reshape(n_etp * experts * capacity, width),
        down_w,
        contract,
        preferred_element_type=jnp.float32,
    )
    gate_f = gate_all.astype(jnp.float32)
    up_f = up_all.astype(jnp.float32)
    sig = jax.nn.sigmoid(gate_f)
    d_gate = (d_hidden * up_f * sig * (1.0 + gate_f * (1.0 - sig))).astype(jnp.bfloat16)
    d_up = (d_hidden * gate_f * sig).astype(jnp.bfloat16)
    both = jnp.concatenate([d_gate, d_up], axis=1)
    term = lax.dot_general(both[:, :hidden], gate_w, contract, preferred_element_type=jnp.float32)
    terms = (
        term + lax.dot_general(both[:, hidden:], up_w, contract, preferred_element_type=jnp.float32)
    ).astype(jnp.bfloat16)
    terms = terms.reshape(n_etp, experts * capacity, width)
    swapped = lax.all_to_all(terms, "expert", split_axis=1, concat_axis=1, tiled=True)
    summed = lax.psum_scatter(swapped, "etp", scatter_dimension=0, tiled=True).astype(jnp.float32)
    returned = summed.reshape(experts * capacity, width).astype(jnp.bfloat16)
    fetched = returned[target].astype(jnp.float32)
    inputs = tokens.astype(jnp.float32)
    d_logit = jnp.sum(inputs * fetched, axis=1) * score * (1.0 - score)
    column = lax.dot_general(
        picked.astype(jnp.bfloat16), router_weight, contract, preferred_element_type=jnp.float32
    )
    token_grad = (score[:, None] * fetched + d_logit[:, None] * column).astype(jnp.bfloat16)
    weighted = jnp.where(picked, d_logit[:, None], 0.0)
    local_terms = jnp.dot(
        inputs.T, weighted, precision=lax.Precision.HIGHEST, preferred_element_type=jnp.float32
    )
    router_grad = lax.psum(local_terms, ("expert", "etp"))
    return (token_grad, router_grad)


def solution(mesh):
    placed = (
        P(("expert", "etp"), None),
        P(("expert", "etp"), None),
        P(),
        P(("expert", "etp"), None),
        P("expert", None, "etp"),
        P("expert", None, "etp"),
        P("expert", None, "etp"),
        P("expert", None, "etp"),
        P("expert", "etp", None),
    )
    return jax.shard_map(
        local,
        mesh=mesh,
        in_specs=placed,
        out_specs=(P(("expert", "etp"), None), P()),
        check_vma=False,
    )
```

profile of v0, /device:TPU:1, one launch (start us, length us, event | category | flops | bytes accessed | tf_op | source)
XLA Modules:
  0.0 812.3 jit_solution(2076231841087327123)
XLA Ops:
  7.2 0.0 all-gather.2.cloned.1.call-start
  7.2 0.8 fusion.28
  8.0 0.1 copy.20
  8.1 0.2 reduce_window_sum.11
  8.3 0.1 copy.21
  8.4 0.7 select_reduce_fusion
  9.1 0.7 fusion.33
  9.7 3.2 scatter_custom_fusion
  12.9 0.0 all-gather.2.cloned.1.call-update
  13.0 0.0 reduce-scatter.2.cloned.1.call-start
  13.0 54.4 %all-gather.2.cloned.1.call-done = bf16[1536,2560]{1,0:T(8,128)(2,1)} async-done(((bf16[192,2560]{1,0:T(8,128)(2,1)}), bf16[1536,2560]{1,0:T(8,128)(2,1)}) %all-gather.2.cloned.1.call-update) | async-done | bytes 7864336 | tf_op jit(solution)/shard_map/all_gather | solution.py:29
  67.4 10.7 %copy.22 = bf16[8,192,2560]{2,0,1:T(8,128)(2,1)} copy(bf16[8,192,2560]{2,1,0:T(8,128)(2,1)} %bitcast.44) | data formatting | bytes 15728640 | tf_op jit(solution)/shard_map/reshape | solution.py:30
  78.1 183.8 %all_to_all.10 = bf16[8,192,2560]{2,0,1:T(8,128)(2,1)} all-to-all(bf16[8,192,2560]{2,0,1:T(8,128)(2,1)} %copy.22), channel_id=1, replica_groups=mesh['expert'=32,'etp'=8] {'expert'}, dimensions={1} | all-to-all | bytes 15728640 | tf_op jit(solution)/shard_map/all_to_all | solution.py:31
  261.9 9.0 %copy.23 = bf16[8,192,2560]{2,1,0:T(8,128)(2,1)} copy(bf16[8,192,2560]{2,0,1:T(8,128)(2,1)} %all_to_all.10) | data formatting | bytes 15728640 | tf_op jit(solution)/shard_map/all_to_all | solution.py:31
  270.8 6.7 fusion.14
  277.6 1.7 copy-done.8
  279.3 9.9 %fusion.12 = f32[1536,2560]{1,0:T(8,128)} fusion(bf16[1,2560,512]{2,1,0:T(8,128)(2,1)S(1)} %copy-done, f32[1536,512]{1,0:T(8,128)S(1)} %fusion.14, bf16[1,1536,512]{2,1,0:T(8,128)(2,1)S(1)} %copy-done.6, bf16[1,1536,512]{2,1,0:T(8,128)(2,1)S(1)} %copy-done.7), kind=kOutput, calls=%fused_computation.21 | convolution fusion | flops 4035969024 | bytes 24641536 | tf_op jit(solution)/shard_map/dot_general | solution.py:44
  289.2 15.2 %add_convert_fusion = bf16[1536,2560]{1,0:T(8,128)(2,1)} fusion(f32[1536,2560]{1,0:T(8,128)} %fusion.12, bf16[1,2560,512]{2,1,0:T(8,128)(2,1)} %param.16, f32[1536,512]{1,0:T(8,128)} %copy-done.8, bf16[1,1536,512]{2,1,0:T(8,128)(2,1)} %param.13), kind=kOutput, calls=%fused_computation.2 | convolution fusion | flops 4039901184 | bytes 30932992 | tf_op jit(solution)/shard_map/dot_general | solution.py:46
  304.5 10.6 %copy.24 = bf16[8,192,2560]{2,0,1:T(8,128)(2,1)} copy(bf16[8,192,2560]{2,1,0:T(8,128)(2,1)} %bitcast.45) | data formatting | bytes 15728640 | tf_op jit(solution)/shard_map/reshape | solution.py:48
  315.1 177.6 %all_to_all.11 = bf16[8,192,2560]{2,0,1:T(8,128)(2,1)} all-to-all(bf16[8,192,2560]{2,0,1:T(8,128)(2,1)} %copy.24), channel_id=1, replica_groups=mesh['expert'=32,'etp'=8] {'expert'}, dimensions={1} | all-to-all | bytes 15728640 | tf_op jit(solution)/shard_map/all_to_all | solution.py:49
  492.6 8.7 %copy.25 = bf16[8,192,2560]{2,1,0:T(8,128)(2,1)} copy(bf16[8,192,2560]{2,0,1:T(8,128)(2,1)} %all_to_all.11) | data formatting | bytes 15728640 | tf_op jit(solution)/shard_map/all_to_all | solution.py:49
  501.4 0.0 all-reduce.2.cloned.1.call-start
  501.5 1.0 copy-done.2
  502.5 0.0 copy-done.3
  502.5 0.3 fusion.24
  502.8 48.4 %reduce-scatter.2.cloned.1.call-done = bf16[1,192,2560]{2,1,0:T(8,128)(2,1)} async-done(((bf16[8,192,2560]{2,1,0:T(8,128)(2,1)}), bf16[1,192,2560]{2,1,0:T(8,128)(2,1)}) %reduce-scatter.2.cloned.1.call-update) | async-done | bytes 983056 | tf_op jit(solution)/shard_map/reduce_scatter | solution.py:50
  551.2 3.9 gather_fusion
  555.2 1.3 fusion.23
  556.5 1.1 convolution_bitcast_fusion
  557.7 2.3 fusion.1
  560.0 244.0 %all-reduce.2.cloned.1.call-done = f32[2560,32]{0,1:T(8,128)} async-done(((f32[2560,32]{0,1:T(8,128)}), f32[2560,32]{0,1:T(8,128)}) %all-reduce.2.cloned.1.call-update) | async-done | bytes 327696 | tf_op jit(solution)/shard_map/psum | solution.py:63
  804.0 1.7 copy.27
  (19 shorter events, 0.1 us)
Async XLA Ops:
  7.2 272.1 %copy-start = (bf16[1,2560,512]{2,1,0:T(8,128)(2,1)S(1)}, bf16[1,2560,512]{2,1,0:T(8,128)(2,1)}, u32[]{:S(2)}) copy-start(bf16[1,2560,512]{2,1,0:T(8,128)(2,1)} %param.15) | copy-start | bytes 7864324
  7.2 60.2 %all-gather.2.cloned.1.call-start = ((), (), s32[]{:S(2)}) async-start(), calls=%async_computation.3 | async-start | bytes 8847360 | tf_op jit(solution)/shard_map/all_gather | solution.py:29
  13.0 538.3 %reduce-scatter.2.cloned.1.call-start = ((), (), s32[]{:S(2)}) async-start(), calls=%async_computation.4 | async-start | bytes 8847360 | tf_op jit(solution)/shard_map/reduce_scatter | solution.py:50
  261.9 9.0 %copy-start.5 = (bf16[1,512,2560]{2,1,0:T(8,128)(2,1)S(1)}, bf16[1,512,2560]{2,1,0:T(8,128)(2,1)}, u32[]{:S(2)}) copy-start(bf16[1,512,2560]{2,1,0:T(8,128)(2,1)} %param.17) | copy-start | bytes 7864324
  270.8 8.5 %copy-start.6 = (bf16[1,1536,512]{2,1,0:T(8,128)(2,1)S(1)}, bf16[1,1536,512]{2,1,0:T(8,128)(2,1)}, u32[]{:S(2)}) copy-start(bf16[1,1536,512]{2,1,0:T(8,128)(2,1)} %param.14) | copy-start | bytes 4718596
  270.8 8.5 %copy-start.7 = (bf16[1,1536,512]{2,1,0:T(8,128)(2,1)S(1)}, bf16[1,1536,512]{2,1,0:T(8,128)(2,1)}, u32[]{:S(2)}) copy-start(bf16[1,1536,512]{2,1,0:T(8,128)(2,1)} %param.13) | copy-start | bytes 4718596
  277.6 1.7 copy-start.8
  501.4 1.1 copy-start.2
  501.4 1.1 copy-start.3
  501.4 1.1 copy-start.4
  501.4 302.6 %all-reduce.2.cloned.1.call-start = ((), (), s32[]{:S(2)}) async-start(), calls=%async_computation.5 | async-start | bytes 655360 | tf_op jit(solution)/shard_map/psum | solution.py:63
  551.2 254.5 %copy-start.1 = (bf16[1,2560,512]{2,1,0:T(8,128)(2,1)S(1)}, bf16[1,2560,512]{2,1,0:T(8,128)(2,1)}, u32[]{:S(2)}) copy-start(bf16[1,2560,512]{2,1,0:T(8,128)(2,1)} %param.15) | copy-start | bytes 7864324
Sparse Core Ops, SparseCore 0:
  13.1 54.2 all-gather.1
  501.5 49.6 reduce-scatter.1
  557.8 246.1 all-reduce.1
where the time goes:
time: 813 us; the launch traced here: 812 us
  blocking collectives  361 us (44%)
  waiting for transfers between devices  347 us (43%)
  local copies, waits for them, and re-layouts  50.8 us (6%)
  matrix products  35.6 us (4%)
  between operations  13.8 us (2%)
    psum x1, waiting for transfers between devices, local(): router_grad = lax.psum(local_terms, ('expert', 'etp'))  244 us
    all_to_all x1, blocking collectives, local(): lax.all_to_all(pooled, 'expert', split_axis=1, concat_axis=1, tiled=True)  184 us
    all_to_all x1, blocking collectives, local(): lax.all_to_all(terms, 'expert', split_axis=1, concat_axis=1, tiled=True)  178 us
    all_gather x1, waiting for transfers between devices, local(): pooled = lax.all_gather(outgoing, 'etp', axis=0, tiled=True)  54.4 us
    reduce_scatter x1, waiting for transfers between devices, local(): lax.psum_scatter(swapped, 'etp', scatter_dimension=0, tiled=True)  48.4 us
  transfers between devices with their start and end apart: 3, of which 3 were waited for; matrix products, arithmetic and copies ran while one was open for 0% of the time, Pallas kernels for 0%

commit v1 on v0

--- a/solution.py
+++ b/solution.py
@@ -60,7 +60,7 @@
     local_terms = jnp.dot(
         inputs.T, weighted, precision=lax.Precision.HIGHEST, preferred_element_type=jnp.float32
     )
-    router_grad = lax.psum(local_terms, ("expert", "etp"))
+    router_grad = lax.psum(lax.psum(local_terms, "expert"), "etp")
     return (token_grad, router_grad)
 
 

time: 813 us -> 776 us (0.954)
  waiting for transfers between devices: 347 us -> 309 us
    psum x1 -> x2, waiting for transfers between devices: 244 us -> 206 us  [local(): router_grad = lax.psum(lax.psum(local_terms, 'expert'), 'etp')]
  transfers between devices with their start and end apart: 3 -> 4, of which waited for: 3 -> 4; matrix products, arithmetic and copies ran while one was open for 0% -> 0% of each run, Pallas kernels for 0% -> 0%
where the time goes in v1:
time: 776 us; the launch traced here: 774 us
  blocking collectives  361 us (47%)
  waiting for transfers between devices  309 us (40%)
  local copies, waits for them, and re-layouts  50.5 us (7%)
  matrix products  35.6 us (5%)
  between operations  13.8 us (2%)
    psum x2, waiting for transfers between devices, local(): router_grad = lax.psum(lax.psum(local_terms, 'expert'), 'etp')  206 us
    all_to_all x1, blocking collectives, local(): lax.all_to_all(pooled, 'expert', split_axis=1, concat_axis=1, tiled=True)  184 us
    all_to_all x1, blocking collectives, local(): lax.all_to_all(terms, 'expert', split_axis=1, concat_axis=1, tiled=True)  178 us
    all_gather x1, waiting for transfers between devices, local(): pooled = lax.all_gather(outgoing, 'etp', axis=0, tiled=True)  54.4 us
    reduce_scatter x1, waiting for transfers between devices, local(): lax.psum_scatter(swapped, 'etp', scatter_dimension=0, tiled=True)  48.4 us
  transfers between devices with their start and end apart: 4, of which 4 were waited for; matrix products, arithmetic and copies ran while one was open for 0% of the time, Pallas kernels for 0%

profile of v1, /device:TPU:1, one launch (start us, length us, event | category | flops | bytes accessed | tf_op | source)
XLA Modules:
  0.0 774.2 jit_solution(5893750816429041148)
XLA Ops:
  7.2 0.0 all-gather.2.cloned.1.call-start
  7.2 0.8 fusion.28
  8.0 0.1 copy.20
  8.1 0.2 reduce_window_sum.11
  8.3 0.1 copy.21
  8.4 0.7 select_reduce_fusion
  9.1 0.7 fusion.33
  9.7 3.2 scatter_custom_fusion
  13.0 0.0 reduce-scatter.2.cloned.1.call-start
  13.0 54.4 %all-gather.2.cloned.1.call-done = bf16[1536,2560]{1,0:T(8,128)(2,1)} async-done(((bf16[192,2560]{1,0:T(8,128)(2,1)}), bf16[1536,2560]{1,0:T(8,128)(2,1)}) %all-gather.2.cloned.1.call-update) | async-done | bytes 7864336 | tf_op jit(solution)/shard_map/all_gather | solution.py:29
  67.4 10.7 %copy.22 = bf16[8,192,2560]{2,0,1:T(8,128)(2,1)} copy(bf16[8,192,2560]{2,1,0:T(8,128)(2,1)} %bitcast.44) | data formatting | bytes 15728640 | tf_op jit(solution)/shard_map/reshape | solution.py:30
  78.1 183.8 %all_to_all.10 = bf16[8,192,2560]{2,0,1:T(8,128)(2,1)} all-to-all(bf16[8,192,2560]{2,0,1:T(8,128)(2,1)} %copy.22), channel_id=1, replica_groups=mesh['expert'=32,'etp'=8] {'expert'}, dimensions={1} | all-to-all | bytes 15728640 | tf_op jit(solution)/shard_map/all_to_all | solution.py:31
  261.9 9.0 %copy.23 = bf16[8,192,2560]{2,1,0:T(8,128)(2,1)} copy(bf16[8,192,2560]{2,0,1:T(8,128)(2,1)} %all_to_all.10) | data formatting | bytes 15728640 | tf_op jit(solution)/shard_map/all_to_all | solution.py:31
  270.8 6.7 fusion.14
  277.6 1.7 copy-done.8
  279.3 9.9 %fusion.12 = f32[1536,2560]{1,0:T(8,128)} fusion(bf16[1,2560,512]{2,1,0:T(8,128)(2,1)S(1)} %copy-done, f32[1536,512]{1,0:T(8,128)S(1)} %fusion.14, bf16[1,1536,512]{2,1,0:T(8,128)(2,1)S(1)} %copy-done.6, bf16[1,1536,512]{2,1,0:T(8,128)(2,1)S(1)} %copy-done.7), kind=kOutput, calls=%fused_computation.21 | convolution fusion | flops 4035969024 | bytes 24641536 | tf_op jit(solution)/shard_map/dot_general | solution.py:44
  289.2 15.2 %add_convert_fusion = bf16[1536,2560]{1,0:T(8,128)(2,1)} fusion(f32[1536,2560]{1,0:T(8,128)} %fusion.12, bf16[1,2560,512]{2,1,0:T(8,128)(2,1)} %param.16, f32[1536,512]{1,0:T(8,128)} %copy-done.8, bf16[1,1536,512]{2,1,0:T(8,128)(2,1)} %param.13), kind=kOutput, calls=%fused_computation.2 | convolution fusion | flops 4039901184 | bytes 30932992 | tf_op jit(solution)/shard_map/dot_general | solution.py:46
  304.5 10.6 %copy.24 = bf16[8,192,2560]{2,0,1:T(8,128)(2,1)} copy(bf16[8,192,2560]{2,1,0:T(8,128)(2,1)} %bitcast.45) | data formatting | bytes 15728640 | tf_op jit(solution)/shard_map/reshape | solution.py:48
  315.1 177.6 %all_to_all.11 = bf16[8,192,2560]{2,0,1:T(8,128)(2,1)} all-to-all(bf16[8,192,2560]{2,0,1:T(8,128)(2,1)} %copy.24), channel_id=1, replica_groups=mesh['expert'=32,'etp'=8] {'expert'}, dimensions={1} | all-to-all | bytes 15728640 | tf_op jit(solution)/shard_map/all_to_all | solution.py:49
  492.6 8.7 %copy.25 = bf16[8,192,2560]{2,1,0:T(8,128)(2,1)} copy(bf16[8,192,2560]{2,0,1:T(8,128)(2,1)} %all_to_all.11) | data formatting | bytes 15728640 | tf_op jit(solution)/shard_map/all_to_all | solution.py:49
  501.4 0.3 all-reduce.3.cloned.1.call-start
  501.7 0.7 copy-done.2
  502.5 0.3 fusion.24
  502.8 48.4 %reduce-scatter.2.cloned.1.call-done = bf16[1,192,2560]{2,1,0:T(8,128)(2,1)} async-done(((bf16[8,192,2560]{2,1,0:T(8,128)(2,1)}), bf16[1,192,2560]{2,1,0:T(8,128)(2,1)}) %reduce-scatter.2.cloned.1.call-update) | async-done | bytes 983056 | tf_op jit(solution)/shard_map/reduce_scatter | solution.py:50
  551.2 3.9 gather_fusion
  555.2 1.3 fusion.23
  556.5 1.1 convolution_bitcast_fusion
  557.7 0.0 all-reduce.5.cloned.1.call-start
  557.7 140.7 %all-reduce.3.cloned.1.call-done = f32[2560,32]{0,1:T(8,128)} async-done(((f32[2560,32]{0,1:T(8,128)}), f32[2560,32]{0,1:T(8,128)}) %all-reduce.3.cloned.1.call-update) | async-done | bytes 327696 | tf_op jit(solution)/shard_map/psum | solution.py:63
  698.4 2.3 fusion.1
  700.7 65.2 %all-reduce.5.cloned.1.call-done = f32[2560,32]{0,1:T(8,128)} async-done(((f32[2560,32]{0,1:T(8,128)}), f32[2560,32]{0,1:T(8,128)}) %all-reduce.5.cloned.1.call-update) | async-done | bytes 327696 | tf_op jit(solution)/shard_map/psum | solution.py:63
  765.9 1.7 copy.28
  (22 shorter events, 0.1 us)
Async XLA Ops:
  7.2 272.1 %copy-start = (bf16[1,2560,512]{2,1,0:T(8,128)(2,1)S(1)}, bf16[1,2560,512]{2,1,0:T(8,128)(2,1)}, u32[]{:S(2)}) copy-start(bf16[1,2560,512]{2,1,0:T(8,128)(2,1)} %param.15) | copy-start | bytes 7864324
  7.2 60.2 %all-gather.2.cloned.1.call-start = ((), (), s32[]{:S(2)}) async-start(), calls=%async_computation.3 | async-start | bytes 8847360 | tf_op jit(solution)/shard_map/all_gather | solution.py:29
  13.0 538.3 %reduce-scatter.2.cloned.1.call-start = ((), (), s32[]{:S(2)}) async-start(), calls=%async_computation.4 | async-start | bytes 8847360 | tf_op jit(solution)/shard_map/reduce_scatter | solution.py:50
  261.9 9.0 %copy-start.5 = (bf16[1,512,2560]{2,1,0:T(8,128)(2,1)S(1)}, bf16[1,512,2560]{2,1,0:T(8,128)(2,1)}, u32[]{:S(2)}) copy-start(bf16[1,512,2560]{2,1,0:T(8,128)(2,1)} %param.17) | copy-start | bytes 7864324
  270.8 8.5 %copy-start.6 = (bf16[1,1536,512]{2,1,0:T(8,128)(2,1)S(1)}, bf16[1,1536,512]{2,1,0:T(8,128)(2,1)}, u32[]{:S(2)}) copy-start(bf16[1,1536,512]{2,1,0:T(8,128)(2,1)} %param.14) | copy-start | bytes 4718596
  270.8 8.5 %copy-start.7 = (bf16[1,1536,512]{2,1,0:T(8,128)(2,1)S(1)}, bf16[1,1536,512]{2,1,0:T(8,128)(2,1)}, u32[]{:S(2)}) copy-start(bf16[1,1536,512]{2,1,0:T(8,128)(2,1)} %param.13) | copy-start | bytes 4718596
  277.6 1.7 copy-start.8
  501.4 1.1 copy-start.2
  501.4 1.1 copy-start.3
  501.4 1.1 copy-start.4
  501.4 197.0 %all-reduce.3.cloned.1.call-start = ((), (), s32[]{:S(2)}) async-start(), calls=%async_computation.5 | async-start | bytes 655360 | tf_op jit(solution)/shard_map/psum | solution.py:63
  551.2 216.4 %copy-start.1 = (bf16[1,2560,512]{2,1,0:T(8,128)(2,1)S(1)}, bf16[1,2560,512]{2,1,0:T(8,128)(2,1)}, u32[]{:S(2)}) copy-start(bf16[1,2560,512]{2,1,0:T(8,128)(2,1)} %param.15) | copy-start | bytes 7864324
  557.7 208.2 %all-reduce.5.cloned.1.call-start = ((), (), s32[]{:S(2)}) async-start(), calls=%async_computation.6 | async-start | bytes 655360 | tf_op jit(solution)/shard_map/psum | solution.py:63
Sparse Core Ops, SparseCore 0:
  13.1 54.2 all-gather.1
  501.5 49.6 reduce-scatter.1
  557.8 140.5 all-reduce.2
  700.7 65.1 all-reduce.4
